TPU v7x, 32 devices: a whole 2x2x4 slice. The times are simulated.
32 devices in a mesh: dp: 8 (over z, x), mp: 4 (over y, core).
Axes of the slice: x: 2, y: 2, z: 4, core: 2. Of those that a mesh axis runs over, the one named last changes fastest.
Arguments:
- encoder_rows: bfloat16 [16384, 768], P('dp'), may hold values from -6 to 6
- piece_extent_sequence: int32 [32, 8], P('dp'), may hold values from 1 to 192, 512 in all within a row
- triple_projection_matrix: bfloat16 [3, 768, 768], P(None, None, 'mp'), may hold values from -0.21875 to 0.21875
- asker_content_shifts: float32 [2, 768], P(None, 'mp'), may hold values from -3 to 3
- mixing_result_matrix: bfloat16 [768, 768], P('mp'), may hold values from -1.75 to 1.75
- mixing_result_offset_vector: float32 [768], replicated, may hold values from -2 to 2
- mixing_normalizer_scale: float32 [768], replicated, may hold values from 0.25 to 1.75
- mixing_normalizer_shift: float32 [768], replicated, may hold values from -2 to 2
- widen_matrix: bfloat16 [768, 3072], P(None, 'mp'), may hold values from -0.21875 to 0.21875
- widen_shift_vector: float32 [3072], P('mp'), may hold values from -3 to 3
- narrow_matrix: bfloat16 [3072, 768], P('mp'), may hold values from -0.15625 to 0.15625
- narrow_shift_vector: float32 [768], replicated, may hold values from -2 to 2
- perceptron_normalizer_scale: float32 [768], replicated, may hold values from 0.25 to 1.75
- perceptron_normalizer_shift: float32 [768], replicated, may hold values from -2 to 2
- document_vectors: bfloat16 [131072, 768], P(('dp', 'mp')), may hold values from -0.36084392 to 0.36084392
- sharpness_factor: float32 [1], replicated, may hold values from 0.4 to 0.52
- correct_document_position: int32 [256], replicated, may hold values from 0 to 131071
- upstream_sensitivity: float32 [16384, 768], P('dp'), may hold values from -0.12 to 0.12
Outputs:
- layer_out: bfloat16 [16384, 768], P('dp')
- seg_loss: float32 [256], replicated
- grad_tokens: float32 [16384, 768], P('dp')
- grad_head_weight: float32 [3, 768, 768], P(None, None, 'mp')
- grad_head_bias: float32 [2, 768], P(None, 'mp')
- grad_out_weight: float32 [768, 768], P('mp')
- grad_out_bias: float32 [768], replicated
- grad_first_gain: float32 [768], replicated
- grad_first_shift: float32 [768], replicated
- grad_up_weight: float32 [768, 3072], P(None, 'mp')
- grad_up_bias: float32 [3072], P('mp')
- grad_down_weight: float32 [3072, 768], P('mp')
- grad_down_bias: float32 [768], replicated
- grad_second_gain: float32 [768], replicated
- grad_second_shift: float32 [768], replicated
- sharpness_derivative: float32 [1], replicated
Inputs may be any that keep to these rules, and one draw needn't show every extreme that they name: `piece_extent_sequence`: each row holds the lengths of the 8 segments of one block in order and sums to 512; the longest segment of each row has exactly 192 tokens.
All inputs are finite; a program needn't handle non-finite values.
Results may differ from a plain program's by a relative error of at most 0.013.
The roundings to bfloat16 on the way count: a program that leaves them out, or rounds other values in their place, can miss the bound.
Values may be sent and summed in bfloat16 or wider, within the bound.
A program may use at most 192 MiB of HBM per device.

v0:
```python
import functools
import math

import jax
import jax.numpy as jnp
from jax import lax
from jax.experimental import pallas as pl
from jax.experimental.pallas import tpu as pltpu
from jax.sharding import PartitionSpec as P

HEAD = 64
F32 = jnp.float32
BF16 = jnp.bfloat16
MESH = pl.DeviceIdType.MESH
norm_epsilon = 1e-05
masked_score = -1e30


def dot(a, b, ca, cb):
    return lax.dot_general(a, b, (((ca,), (cb,)), ((), ())), preferred_element_type=F32)


def norm_stats(resid):
    centre = jnp.mean(resid, axis=-1, keepdims=True)
    centred = resid - centre
    spread = jnp.mean(centred * centred, axis=-1, keepdims=True)
    inv = lax.rsqrt(spread + norm_epsilon)
    return centred * inv, inv


def norm_back(d_out, normed, inv, gain):
    e = d_out * gain
    return inv * (
        e - jnp.mean(e, axis=-1, keepdims=True) - normed * jnp.mean(e * normed, axis=-1, keepdims=True)
    )


def flip(index, step):
    return index + step * (1 - 2 * lax.rem(index // step, 2))


def retrieval_kernel(
    ndp, nmp, query_ref, own_ref, docs_hbm, gold_ref, sharp_ref, dq_ref, loss_ref, ds_ref, layer,
    queries, docs, low, stats, columns, part_u, part_g, send, got, doc_sem, q_send, q_recv, s_send, s_recv, d_send, d_recv,
    l_s, l_r, own_sem,
):
    n = ndp * nmp
    own = query_ref.shape[0]
    nseg = gold_ref.shape[1]
    tile = 256 if nseg <= 256 else 128
    dp, mp = lax.axis_index("dp"), lax.axis_index("mp")
    me = dp * nmp + mp
    load = pltpu.make_async_copy(docs_hbm, docs, doc_sem)
    load.start()
    barrier = pltpu.get_barrier_semaphore()

    def device(step):
        other = lax.rem(me + step, n)
        return other, (other // nmp, lax.rem(other, nmp))

    @pl.loop(1, n)
    def _(step):
        _, where = device(step)
        pl.semaphore_signal(barrier, inc=1, device_id=where, device_id_type=MESH)

    pl.semaphore_wait(barrier, n - 1)

    def push(source, target, send_sems, recv_sems):
        @pl.loop(1, n)
        def _(step):
            other, where = device(step)
            pltpu.make_async_remote_copy(
                source(other), target, send_sems.at[step], recv_sems.at[step], device_id=where, device_id_type=MESH
            ).start()

    def drain(source, target, send_sems, recv_sems):
        @pl.loop(1, n)
        def _(step):
            other, where = device(step)
            copy = pltpu.make_async_remote_copy(
                source(other), target, send_sems.at[step], recv_sems.at[step], device_id=where, device_id_type=MESH
            )
            copy.wait()

    push(lambda other: query_ref, queries.at[me], q_send, q_recv)
    queries[me] = query_ref[...]
    drain(lambda other: query_ref, queries.at[me], q_send, q_recv)
    near, far, across = (dp, flip(mp, 1)), (dp, flip(mp, 2)), flip(mp, 2)

    def spread(source, target, i, where):
        return pltpu.make_async_remote_copy(
            source, target, l_s.at[i], l_r.at[i], device_id=where, device_id_type=MESH
        )

    to_near = spread(own_ref, layer.at[mp], 0, near)
    to_far, to_pass, first = [], [], 0
    for i, part in enumerate((7, 6, 3)):
        strip = pl.ds(first, own_ref.shape[0] * part // 16)
        first += own_ref.shape[0] * part // 16
        passed = layer.at[across, strip]
        to_far.append(spread(own_ref.at[strip], layer.at[mp, strip], 1 + i, far))
        to_pass.append(spread(passed, passed, 4 + i, near))
    keep = pltpu.make_async_copy(own_ref, layer.at[mp], own_sem)
    to_far[0].start()
    to_near.start()
    keep.start()
    load.wait()

    sharp = sharp_ref[0]
    offset = me * docs.shape[0]
    ids = lax.broadcasted_iota(jnp.int32, (tile, docs.shape[0]), 1).astype(F32)
    columns[...] = jnp.broadcast_to((gold_ref[...] - offset).astype(F32), (128, nseg)).T
    lane = lax.broadcasted_iota(jnp.int32, (tile, 128), 1)
    per = tile // own

    @pl.loop(0, nseg // tile)
    def _(i):
        span = pl.ds(pl.multiple_of(i * tile, tile), tile)
        q = queries[pl.ds(i * per, per)].reshape(tile, queries.shape[2])
        logit = lax.dot_general(q, docs[...], (((1,), (1,)), ((), ())), preferred_element_type=F32) / sharp
        match = ids == columns[span, 0:1]
        top = jnp.max(logit, axis=1, keepdims=True)
        expo = jnp.exp(logit - top)
        total = jnp.sum(expo, axis=1, keepdims=True)
        tilt = jnp.sum(expo * logit, axis=1, keepdims=True)
        gold = jnp.sum(jnp.where(match, logit, 0.0), axis=1, keepdims=True)
        packed = jnp.where(lane == 0, top, jnp.where(lane == 1, total, jnp.where(lane == 2, tilt, gold)))
        stats[me, :, span] = packed.T[:4]
        low[span, :] = jnp.where(match, 0.0, expo).astype(BF16)

    push(lambda other: stats.at[me], stats.at[me], s_send, s_recv)
    to_far[1].start()

    @pl.loop(0, nseg // tile)
    def _(i):
        span = pl.ds(pl.multiple_of(i * tile, tile), tile)
        part_u[span, :] = jnp.dot(low[span, :], docs[...], preferred_element_type=F32)
        match = ids == columns[span, 0:1]
        part_g[span, :] = jnp.dot(
            match.astype(F32).astype(BF16), docs[...], preferred_element_type=F32
        ).astype(BF16)

    drain(lambda other: stats.at[me], stats.at[me], s_send, s_recv)
    to_far[0].wait_recv()
    to_pass[0].start()

    tops = stats[:, 0, :]
    top = jnp.max(tops, axis=0, keepdims=True)
    share = jnp.exp(tops - top)
    total = jnp.sum(stats[:, 1, :] * share, axis=0, keepdims=True)
    tilt = jnp.sum(stats[:, 2, :] * share, axis=0, keepdims=True)
    gold = jnp.sum(stats[:, 3, :], axis=0, keepdims=True)
    lse = top + jnp.log(total)
    loss_ref[...] = lse - gold
    ds_ref[...] = -jnp.sum(tilt / total - gold, axis=1, keepdims=True) / sharp
    scale = jnp.exp(stats[me, 0:1, :] - lse) / sharp
    gold_scale = (jnp.exp(gold - lse) - 1.0) / sharp
    row = lax.broadcasted_iota(jnp.int32, (128, nseg), 0)
    columns[...] = jnp.where(row == 0, scale, gold_scale).T

    @pl.loop(0, nseg // tile)
    def _(i):
        span = pl.ds(pl.multiple_of(i * tile, tile), tile)
        value = part_u[span, :] * columns[span, 0:1] + part_g[span, :].astype(F32) * columns[span, 1:2]
        send[pl.ds(i * per, per)] = value.astype(BF16).reshape(per, own, value.shape[1])

    push(lambda other: send.at[other], got.at[me], d_send, d_recv)
    to_far[2].start()
    to_far[1].wait_recv()
    to_pass[1].start()
    got[me] = send[me]
    drain(lambda other: send.at[other], got.at[me], d_send, d_recv)
    dq_ref[...] = jnp.sum(got[...].astype(F32), axis=0)
    to_far[2].wait_recv()
    to_pass[2].start()
    to_near.wait()
    for copy in to_far:
        copy.wait_send()
    for copy in to_pass:
        copy.wait()
    keep.wait()


def retrieval(query, own_out, docs, gold, sharp, ndp, nmp):
    n = ndp * nmp
    own, width = query.shape
    nseg = gold.shape[1]
    vmem = pl.BlockSpec(memory_space=pltpu.VMEM)
    return pl.pallas_call(
        functools.partial(retrieval_kernel, ndp, nmp),
        out_shape=(
            jax.ShapeDtypeStruct((own, width), F32),
            jax.ShapeDtypeStruct((1, nseg), F32),
            jax.ShapeDtypeStruct((1, 1), F32),
            jax.ShapeDtypeStruct((nmp,) + own_out.shape, BF16),
        ),
        in_specs=[vmem, vmem, pl.BlockSpec(memory_space=pl.ANY), vmem, pl.BlockSpec(memory_space=pltpu.SMEM)],
        out_specs=(vmem, vmem, vmem, pl.BlockSpec(memory_space=pl.ANY)),
        scratch_shapes=[
            pltpu.VMEM((n, own, width), BF16),
            pltpu.VMEM(docs.shape, BF16),
            pltpu.VMEM((nseg, docs.shape[0]), BF16),
            pltpu.VMEM((n, 4, nseg), F32),
            pltpu.VMEM((nseg, 128), F32),
            pltpu.VMEM((nseg, width), F32),
            pltpu.VMEM((nseg, width), BF16),
            pltpu.VMEM((n, own, width), BF16),
            pltpu.VMEM((n, own, width), BF16),
            pltpu.SemaphoreType.DMA,
        ]
        + [pltpu.SemaphoreType.DMA((n,))] * 6
        + [pltpu.SemaphoreType.DMA((7,))] * 2
        + [pltpu.SemaphoreType.DMA],
        compiler_params=pltpu.CompilerParams(
            collective_id=0, has_side_effects=True, vmem_limit_bytes=60 * 2**20
        ),
        name="retrieval",
    )(query, own_out, docs, gold, sharp)


def gelu_with_slope(u):
    z = jnp.abs(u) * (0.5**0.5)
    t = 1.0 / (1.0 + 0.5 * z)
    poly = 0.17087277
    for c in (
        -0.82215223, 1.48851587, -1.13520398, 0.27886807, -0.18628806, 0.09678418, 0.37409196, 1.00002368,
    ):
        poly = poly * t + c
    square = z * z
    tail = 0.5 * t * jnp.exp(poly * t - 1.26551223 - square)
    cdf = jnp.where(u < 0, tail, 1.0 - tail)
    return u * cdf, cdf + u * (jnp.exp(-square) * ((2 * math.pi) ** -0.5))


def encode_kernel(nmp, block, *refs):
    (
        rows_hbm, extents, w_qkv, w_out, w_up, w_down, small_ref, *vectors,
    ) = refs[:13]
    out_bias, gain1, shift1, down_bias, gain2, shift2 = (v[...][None] for v in vectors)
    (
        qkv_o, mixed_o, n1_o, inv1_o, n2_o, inv2_o, low_o, act_o, slope_o, w_qkv_o, w_out_o, w_up_o, w_down_o,
        own_o, query_o, x_o,
    ) = refs[13:29]
    (
        x, qkv, mixed, n1, n2, h1_low, act, slope, all_qkv, all_out, all_up, all_down, small, total,
        fill_sem, save_sem, n_s, n_r, m_s, m_r, y_s, y_r, f_s, f_r, g_s, g_r, h_s, h_r, sm_s, sm_r,
    ) = refs[29:]
    dp, mp = lax.axis_index("dp"), lax.axis_index("mp")
    near, far, side = (dp, flip(mp, 1)), (dp, flip(mp, 2)), (flip(dp, 1), mp)
    b = lax.rem(dp, 2)
    rows = x.shape[0]
    feat = w_out.shape[0] * w_out.shape[1]
    scale = HEAD ** (-0.5)

    own_rows = rows_hbm.at[pl.ds(pl.multiple_of(mp * rows, rows), rows)]
    fills = [
        pltpu.make_async_copy(source, target, fill_sem.at[i])
        for i, (source, target) in enumerate(
            [
                (own_rows, x), (w_qkv, all_qkv.at[0]), (w_out, all_out.at[0]), (w_up, all_up.at[0]),
                (w_down, all_down.at[0]),
            ]
        )
    ]
    for copy in fills:
        copy.start()
    barrier = pltpu.get_barrier_semaphore()
    for where in (near, far, side):
        pl.semaphore_signal(barrier, inc=1, device_id=where, device_id_type=MESH)
    pl.semaphore_wait(barrier, 3)

    def remote(source, target, send, recv, where):
        return pltpu.make_async_remote_copy(source, target, send, recv, device_id=where, device_id_type=MESH)

    pieces = [(w_qkv.at[k], all_qkv, k) for k in range(3)] + [(w_out, all_out, None)]
    pieces += [(w_up.at[s], all_up, s) for s in range(w_up.shape[0])]
    pieces += [(w_down.at[s], all_down, s) for s in range(w_down.shape[0])]
    count = len(pieces)

    def slot(i, r):
        _, held, s = pieces[i]
        return held.at[r] if s is None else held.at[r, s]

    near_own = [remote(pieces[i][0], slot(i, 1), n_s.at[i], n_r.at[i], near) for i in range(count)]
    far_own = [remote(pieces[i][0].at[b], slot(i, 2).at[b], y_s.at[i], y_r.at[i], far) for i in range(count)]
    pass_side = [remote(slot(i, 2).at[b], slot(i, 2).at[b], f_s.at[i], f_r.at[i], side) for i in range(count)]
    pass_near = [remote(slot(i, 2).at[b], slot(i, 3).at[b], g_s.at[i], g_r.at[i], near) for i in range(count)]
    pass_other = [
        remote(slot(i, 2).at[1 - b], slot(i, 3).at[1 - b], h_s.at[i], h_r.at[i], near) for i in range(count)
    ]
    small_near = remote(small_ref, small.at[1], sm_s.at[0], sm_r.at[0], near)
    small_far = remote(small_ref, small.at[2], sm_s.at[1], sm_r.at[1], far)
    small_pass = remote(small.at[2], small.at[3], sm_s.at[2], sm_r.at[2], near)

    small_near.start()
    small_far.start()
    for i in range(count):
        far_own[i].start()
        near_own[i].start()
    small[0] = small_ref[...]
    by_quarter = [
        (qkv, qkv_o), (mixed, mixed_o), (act, act_o), (slope, slope_o), (all_qkv, w_qkv_o), (all_out, w_out_o),
        (all_up, w_up_o), (all_down, w_down_o),
    ]
    at_once = [(x, x_o), (n1, n1_o), (h1_low, low_o), (n2, n2_o)]

    def save(i, r):
        source, target = by_quarter[i]
        return pltpu.make_async_copy(source.at[r], target.at[r], save_sem.at[4 * i + r])

    def save_whole(i):
        source, target = at_once[i]
        return pltpu.make_async_copy(source, target, save_sem.at[4 * len(by_quarter) + i])

    def relay(i):
        far_own[i].wait_recv()
        pass_side[i].start()
        pass_near[i].start()

    def relay_other(i):
        pass_side[i].wait_recv()
        pass_other[i].start()

    def last_arrived(i):
        pass_near[i].wait_recv()
        pass_other[i].wait_recv()

    iota_row = lax.broadcasted_iota(jnp.int32, (1, rows), 1)
    iota_col = lax.broadcasted_iota(jnp.int32, (rows, 1), 0)
    nblk = rows // block
    nseg = extents.shape[1]
    seg_row, seg_col = jnp.zeros_like(iota_row), jnp.zeros_like(iota_col)
    starts = []
    for i in range(nblk):
        end = jnp.int32(i * block)
        for j in range(nseg):
            starts.append(end)
            end = end + extents[mp * nblk + i, j]
            seg_row = seg_row + (iota_row >= end).astype(jnp.int32)
            seg_col = seg_col + (iota_col >= end).astype(jnp.int32)
    wide = x.shape[1]
    ups, downs = range(4, 4 + w_up.shape[0]), range(4 + w_up.shape[0], count)

    def head(r, h):
        lanes = slice(h * HEAD, (h + 1) * HEAD)
        q = qkv[r, 0, :, lanes] * BF16(scale)
        scores = dot(q, qkv[r, 1, :, lanes], 1, 1)
        scores = jnp.where(seg_col == seg_row, scores, masked_score)
        expo = jnp.exp(scores - jnp.max(scores, axis=1, keepdims=True))
        probs = (expo * (1.0 / jnp.sum(expo, axis=1, keepdims=True))).astype(BF16)
        mixed[r, :, lanes] = jnp.dot(probs, qkv[r, 2, :, lanes], preferred_element_type=F32).astype(BF16)

    def both(i):
        relay(i)
        relay_other(i - 1)

    def on(r, at, *steps):
        @pl.when(r == at)
        def _():
            for step in steps:
                step()

    near_in = lambda group: [near_own[i].wait_recv for i in group]
    last_in = lambda group: [functools.partial(last_arrived, i) for i in group]
    do = functools.partial
    fills[0].wait()
    fills[1].wait()
    save_whole(0).start()

    @pl.loop(0, nmp)
    def _(r):
        on(r, 1, small_near.wait_recv, *near_in(range(3)))
        on(
            r, 2, small_far.wait_recv, small_pass.start, do(relay, 0), do(relay, 1), do(relay_other, 0), do(relay, 2),
            do(relay_other, 1), do(relay, 3), do(relay_other, 2),
        )
        on(r, 3, small_pass.wait_recv, *last_in(range(3)))
        for k in range(3):
            value = dot(x[...], all_qkv[r, k].reshape(feat, wide), 1, 1)
            if k == 0:
                value = value + small[r, 0:1, :feat]
            if k == 2:
                value = value + small[r, 1:2, :feat]
            qkv[r, k] = value.astype(BF16)
        save(0, r).start()
        save(4, r).start()
        head(r, 0)
        on(r, 2, do(relay_other, 3))
        on(r, 3, do(both, 5))
        head(r, 1)
        on(r, 2, do(relay, 4))
        for h in range(2, feat // HEAD):
            head(r, h)
        save(1, r).start()

    fills[2].wait()
    near_own[3].wait_recv()
    last_arrived(3)
    total[...] = x[...].astype(F32) + out_bias

    @pl.loop(0, nmp)
    def _(r):
        total[...] += jnp.dot(mixed[r], all_out[r].reshape(feat, wide), preferred_element_type=F32)
        save(5, r).start()

    tile = 128

    @pl.loop(0, rows // tile)
    def _(t):
        span = pl.ds(pl.multiple_of(t * tile, tile), tile)
        normed, inv = norm_stats(total[span])
        n1[span] = normed
        inv1_o[span] = jnp.broadcast_to(inv, (tile, inv1_o.shape[1]))
        h1 = normed * gain1 + shift1
        total[span] = h1 + down_bias
        h1_low[span] = h1.astype(BF16)

    save_whole(1).start()
    save_whole(2).start()
    both(6)
    fills[3].wait()
    fills[4].wait()

    @pl.loop(0, nmp)
    def _(r):
        on(r, 1, *near_in(ups))
        on(r, 3, *last_in(ups))
        upper = jnp.dot(h1_low[...], all_up[r].reshape(wide, -1), preferred_element_type=F32) + small[r, 2:3, :]
        value, gradient = gelu_with_slope(upper)
        act[r] = value.astype(BF16)
        slope[r] = gradient.astype(BF16)
        for i in (2, 3, 6):
            save(i, r).start()
        on(r, 0, do(both, 7))
        on(r, 1, do(both, 8), *near_in(downs))
        on(r, 2, do(both, 9), do(relay_other, 9))
        on(r, 3, *last_in(downs))
        total[...] += jnp.dot(act[r], all_down[r].reshape(-1, wide), preferred_element_type=F32)
        save(7, r).start()

    @pl.loop(0, rows // tile)
    def _(t):
        span = pl.ds(pl.multiple_of(t * tile, tile), tile)
        normed, inv = norm_stats(total[span])
        n2[span] = normed
        inv2_o[span] = jnp.broadcast_to(inv, (tile, inv2_o.shape[1]))
        own_o[span] = (normed * gain2 + shift2).astype(BF16)

    save_whole(3).start()
    line = lax.broadcasted_iota(jnp.int32, (len(starts), rows), 0)
    first = jnp.zeros((len(starts), rows), jnp.int32)
    for j, start in enumerate(starts):
        first = jnp.where(line == j, start, first)
    pick = (lax.broadcasted_iota(jnp.int32, first.shape, 1) == first).astype(F32).astype(BF16)
    query_o[...] = jnp.dot(pick, own_o[...], preferred_element_type=F32).astype(BF16)
    for i in range(len(at_once)):
        save_whole(i).wait()

    @pl.loop(0, nmp)
    def _(r):
        for i in range(len(by_quarter)):
            save(i, r).wait()

    for copy in near_own + far_own + pass_side + pass_near + pass_other + [small_near, small_far, small_pass]:
        copy.wait_send()


STRIPS = 3


def encode(
    encoder_rows, extents, w_qkv, w_out, w_up, w_down, small, out_bias, gain1, shift1, down_bias, gain2, shift2,
    block, nmp,
):
    rows = encoder_rows.shape[0] // nmp
    wide = encoder_rows.shape[1]
    feat, hidden = w_qkv.shape[1], w_up.shape[1]
    nseg = extents.shape[0] * extents.shape[1] // nmp
    cut_qkv = w_qkv.reshape(3, 2, feat // 2, wide)
    cut_out = w_out.reshape(2, feat // 2, wide)
    cut_up = w_up.reshape(STRIPS, 2, wide // (2 * STRIPS), hidden)
    cut_down = w_down.reshape(STRIPS, 2, hidden // (2 * STRIPS), wide)
    vmem, anywhere = pl.BlockSpec(memory_space=pltpu.VMEM), pl.BlockSpec(memory_space=pl.ANY)
    sds = jax.ShapeDtypeStruct
    dma = pltpu.SemaphoreType.DMA
    every = lambda a: (nmp,) + a.shape
    held = [
        sds((nmp, 3, rows, feat), BF16),
        sds((nmp, rows, feat), BF16),
        sds((rows, wide), F32),
        sds((rows, 128), F32),
        sds((rows, wide), F32),
        sds((rows, 128), F32),
        sds((rows, wide), BF16),
        sds((nmp, rows, hidden), BF16),
        sds((nmp, rows, hidden), BF16),
        sds(every(cut_qkv), BF16),
        sds(every(cut_out), BF16),
        sds(every(cut_up), BF16),
        sds(every(cut_down), BF16),
        sds((rows, wide), BF16),
        sds((nseg, wide), BF16),
        sds((rows, wide), BF16),
    ]
    count = 4 + 2 * STRIPS
    scratch = [
        pltpu.VMEM((rows, wide), BF16),
        pltpu.VMEM(held[0].shape, BF16),
        pltpu.VMEM(held[1].shape, BF16),
        pltpu.VMEM((rows, wide), F32),
        pltpu.VMEM((rows, wide), F32),
        pltpu.VMEM((rows, wide), BF16),
        pltpu.VMEM(held[7].shape, BF16),
        pltpu.VMEM(held[8].shape, BF16),
    ]
    scratch += [pltpu.VMEM(h.shape, BF16) for h in held[9:13]]
    scratch += [pltpu.VMEM(every(small), F32), pltpu.VMEM((rows, wide), F32), dma((5,)), dma((36,))]
    scratch += [dma((count,))] * 12 + [dma((3,))] * 2
    outs = pl.pallas_call(
        functools.partial(encode_kernel, nmp, block),
        out_shape=tuple(held),
        in_specs=[anywhere, pl.BlockSpec(memory_space=pltpu.SMEM)] + [anywhere] * 4 + [vmem] * 7,
        out_specs=tuple(vmem if i in (3, 5, 13, 14) else anywhere for i in range(len(held))),
        scratch_shapes=scratch,
        compiler_params=pltpu.CompilerParams(collective_id=2, has_side_effects=True, vmem_limit_bytes=62 * 2**20),
        name="encode",
    )(encoder_rows, extents, cut_qkv, cut_out, cut_up, cut_down, small, out_bias, gain1, shift1, down_bias, gain2, shift2)
    outs = list(outs)
    outs[9] = outs[9].reshape(nmp, 3, feat, wide)
    outs[10] = outs[10].reshape(nmp, feat, wide)
    outs[11] = outs[11].reshape(nmp, wide, hidden)
    outs[12] = outs[12].reshape(nmp, hidden, wide)
    return outs


PIECES = 8
CHUNKS = 6
KINDS = 3
LAGS = (0, 2, 3, 5, 6, 8, 10)


def backward_kernel(ndp, nmp, block, *refs):
    (
        d_query, extents, gain1, gain2, upstream_h, n1_h, inv1_h, n2_h, inv2_h, low_h, act_h, slope_h, up_h, down_h,
        qkv_h, mixed_h, w_out_h, w_qkv_h, x_h,
    ) = refs[:19]
    out, vec_out, tok = refs[19:22]
    (
        total, n1, inv1, n2, inv2, h1_low, x, act, slope, w_up, w_down, qkv, mixed, w_out, w_qkv,
        d_ffn, d_attn, d_proj, low_tok, parts, vec, near, got_y, got_x, got_1, got_2, got_e,
        vec_a, vec_b, vec_s, vec_r,
        load_sem, ffn_sem, attn_sem, a_s, a_r, y_s, y_r, x_s, x_r, p_s, p_r, q_s, q_r, e_s, e_r,
        gq_s, gq_r, gp_s, gp_r, gx_s, gx_r, va_s, va_r, v_s, v_r, t_s, t_r, own_sem,
    ) = refs[22:]
    count = KINDS * CHUNKS
    bits = ndp.bit_length() - 1
    extra = bits - 3
    rows, wide = total.shape
    feat = mixed.shape[2]
    hidden = act.shape[2]
    dp, mp = lax.axis_index("dp"), lax.axis_index("mp")
    near_dev, far_dev = (dp, flip(mp, 1)), (dp, flip(mp, 2))
    dp_dev = [(flip(dp, 1 << b), mp) for b in range(bits)]
    b0, b1, b2 = (lax.rem(dp // (1 << b), 2) for b in range(3))
    ident = b0 * 4 + b1 * 2 + b2
    gain1, gain2 = gain1[...][None], gain2[...][None]

    own_rows = upstream_h.at[pl.ds(pl.multiple_of(mp * rows, rows), rows)]
    loads = [
        pltpu.make_async_copy(source, target, load_sem.at[i])
        for i, (source, target) in enumerate(
            [
                (own_rows, total), (n2_h, n2), (inv2_h, inv2), (act_h, act), (low_h, h1_low), (n1_h, n1),
                (inv1_h, inv1), (x_h, x),
            ]
        )
    ]

    def ffn_loads(i):
        r, slot = 3 - i, lax.rem(i, 2)
        return [
            pltpu.make_async_copy(source.at[r], target.at[slot], ffn_sem.at[slot, j])
            for j, (source, target) in enumerate([(down_h, w_down), (slope_h, slope), (up_h, w_up)])
        ]

    def attn_loads(i):
        r, slot = 3 - i, lax.rem(i, 2)
        return [
            pltpu.make_async_copy(source.at[r], target.at[slot], attn_sem.at[slot, j])
            for j, (source, target) in enumerate([(w_out_h, w_out), (qkv_h, qkv), (mixed_h, mixed), (w_qkv_h, w_qkv)])
        ]

    for copy in loads + ffn_loads(0):
        copy.start()
    barrier = pltpu.get_barrier_semaphore()
    for where in [near_dev, far_dev] + dp_dev:
        pl.semaphore_signal(barrier, inc=1, device_id=where, device_id_type=MESH)
    pl.semaphore_wait(barrier, 2 + bits)

    def remote(source, target, send, recv, where):
        return pltpu.make_async_remote_copy(source, target, send, recv, device_id=where, device_id_type=MESH)

    def part(c, r, first=0, many=PIECES):
        k = c // CHUNKS
        return parts.at[k, r, pl.ds((c - k * CHUNKS) * PIECES + first, many)]

    def near_copy(k, j):
        return remote(parts.at[k, 2 * j + 1], near.at[k, j], a_s.at[2 * k + j], a_r.at[2 * k + j], near_dev)

    def far_copy(c):
        return remote(part(c, 2), got_y.at[c], y_s.at[c], y_r.at[c], far_dev)

    def x_copy(c):
        return remote(part(c, 0, (1 - b0) * 4, 4), got_x.at[c], x_s.at[c], x_r.at[c], dp_dev[0])

    def p_copy(c):
        return remote(part(c, 0, b0 * 4 + (1 - b1) * 2, 2), got_1.at[c], p_s.at[c], p_r.at[c], dp_dev[1])

    def q_copy(c):
        return remote(part(c, 0, ident + 1 - 2 * b2, 1), got_2.at[c], q_s.at[c], q_r.at[c], dp_dev[2])

    def e_copy(c, e):
        return remote(part(c, 0, ident, 1), got_e.at[e, c], e_s.at[e, c], e_r.at[e, c], dp_dev[3 + e])

    def gq_copy(c):
        held = out.at[c, b0, b1, b2]
        return remote(held, held, gq_s.at[c], gq_r.at[c], dp_dev[2])

    def gp_copy(c):
        held = out.at[c, b0, b1]
        return remote(held, held, gp_s.at[c], gp_r.at[c], dp_dev[1])

    def gx_copy(c):
        held = out.at[c, b0]
        return remote(held, held, gx_s.at[c], gx_r.at[c], dp_dev[0])

    vec_near = [remote(vec.at[2 * j + 1], vec_a.at[j], va_s.at[j], va_r.at[j], near_dev) for j in range(2)]
    vec_far = remote(vec_b, vec_r.at[0], v_s.at[0], v_r.at[0], far_dev)
    vec_dp = [remote(vec_s.at[b], vec_r.at[1 + b], v_s.at[1 + b], v_r.at[1 + b], dp_dev[b]) for b in range(bits)]
    across = flip(mp, 2)
    tok_near = remote(low_tok, tok.at[mp], t_s.at[0], t_r.at[0], near_dev)
    tok_far = remote(low_tok, tok.at[mp], t_s.at[1], t_r.at[1], far_dev)
    tok_pass = remote(tok.at[across], tok.at[across], t_s.at[2], t_r.at[2], near_dev)
    tok_own = pltpu.make_async_copy(low_tok, tok.at[mp], own_sem)

    def add(a, b):
        return (a.astype(F32) + b.astype(F32)).astype(BF16)

    def exchange(k, r):
        j = r // 2

        @pl.when(lax.rem(r, 2) == 1)
        def _():
            near_copy(k, j).start()

        @pl.when(lax.rem(r, 2) == 0)
        def _():
            near_copy(k, j).wait_recv()

            @pl.loop(0, CHUNKS)
            def _(i):
                span = pl.ds(i * PIECES, PIECES)
                parts[k, r, span] = add(parts[k, r, span], near[k, j, span])

                @pl.when(j == 1)
                def _():
                    far_copy(k * CHUNKS + i).start()

    def tick(i):
        def at(lag, do):
            @pl.when((i >= lag) & (i - lag < count))
            def _():
                do(i - lag)

        def update(c, first, many, got):
            target = part(c, 0, first, many)
            target[...] = add(target[...], got[c])

        @functools.partial(at, LAGS[6] + extra)
        def _(c):
            gx_copy(c).wait_recv()

        @functools.partial(at, LAGS[5] + extra)
        def _(c):
            gp_copy(c).wait_recv()
            gx_copy(c).start()

        @functools.partial(at, LAGS[4] + extra)
        def _(c):
            gq_copy(c).wait_recv()
            gp_copy(c).start()

        for e in reversed(range(extra)):
            @functools.partial(at, LAGS[3] + 1 + e)
            def _(c, e=e):
                e_copy(c, e).wait()
                update(c, ident, 1, got_e.at[e])
                if e + 1 < extra:
                    e_copy(c, e + 1).start()
                else:
                    out[c, b0, b1, b2] = part(c, 0, ident, 1)[0]
                    gq_copy(c).start()

        @functools.partial(at, LAGS[3])
        def _(c):
            q_copy(c).wait_recv()
            if extra:
                update(c, ident, 1, got_2)
                e_copy(c, 0).start()
            else:
                out[c, b0, b1, b2] = add(part(c, 0, ident, 1)[0], got_2[c, 0])
                gq_copy(c).start()

        @functools.partial(at, LAGS[2])
        def _(c):
            p_copy(c).wait_recv()
            update(c, b0 * 4 + b1 * 2, 2, got_1)
            q_copy(c).start()

        @functools.partial(at, LAGS[1])
        def _(c):
            x_copy(c).wait_recv()
            update(c, b0 * 4, 4, got_x)
            p_copy(c).start()

        @functools.partial(at, 0)
        def _(c):
            far_copy(c).wait_recv()
            update(c, 0, PIECES, got_y)
            x_copy(c).start()

    tile = 128
    nblk = rows // block
    nseg = extents.shape[1]
    vec[...] = jnp.zeros_like(vec)
    for copy in loads[:3]:
        copy.wait()

    def count_up(row, value):
        vec[0, row : row + 1] += jnp.sum(value, axis=0, keepdims=True)

    @pl.loop(0, rows // tile)
    def _(t):
        span = pl.ds(pl.multiple_of(t * tile, tile), tile)
        line = lax.broadcasted_iota(jnp.int32, (tile, 1), 0) + t * tile
        d_h2 = total[span]
        for i in range(nblk):
            start = jnp.int32(i * block)
            for j in range(nseg):
                d_h2 = d_h2 + jnp.where(line == start, d_query[i * nseg + j, :][None], 0.0)
                start = start + extents[mp * nblk + i, j]
        normed = n2[span]
        count_up(5, d_h2)
        count_up(4, d_h2 * normed)
        d_r2 = norm_back(d_h2, normed, inv2[span, 0:1], gain2)
        count_up(3, d_r2)
        d_ffn[span] = d_r2.astype(BF16)
        total[span] = d_r2

    def store(k, r, first, value):
        pieces = value.shape[0] // parts.shape[3]
        parts[k, r, first : first + pieces] = value.astype(BF16).reshape(pieces, parts.shape[3], wide)

    loads[3].wait()

    @pl.loop(0, nmp)
    def _(i):
        r = 3 - i
        store(0, r, 0, dot(act[r], d_ffn[...], 0, 0))
        exchange(0, r)

    for copy in loads[4:]:
        copy.wait()
    for copy in attn_loads(0):
        copy.start()

    @pl.loop(0, nmp)
    def _(i):
        r, slot = 3 - i, lax.rem(i, 2)
        for copy in ffn_loads(i):
            copy.wait()

        @pl.when(i + 1 < nmp)
        def _():
            for copy in ffn_loads(i + 1):
                copy.start()

        d_up = (dot(d_ffn[...], w_down[slot], 1, 1) * slope[slot].astype(F32)).astype(BF16)
        vec[r, 7:8, :hidden] = jnp.sum(d_up.astype(F32), axis=0, keepdims=True)
        store(1, r, 0, dot(h1_low[...], d_up, 0, 0))
        exchange(1, r)
        total[...] += dot(d_up, w_up[slot], 1, 1)

        @pl.loop(i - (i + 2) // 3, i + i // 3)
        def _(n):
            tick(n)

    @pl.loop(0, rows // tile)
    def _(t):
        span = pl.ds(pl.multiple_of(t * tile, tile), tile)
        d_h1 = total[span]
        normed = n1[span]
        count_up(2, d_h1)
        count_up(1, d_h1 * normed)
        d_r1 = norm_back(d_h1, normed, inv1[span, 0:1], gain1)
        count_up(0, d_r1)
        d_attn[span] = d_r1.astype(BF16)
        total[span] = d_r1

    for r in range(1, nmp):
        vec[r, 0:6] = vec[0, 0:6]

    iota_row = lax.broadcasted_iota(jnp.int32, (1, rows), 1)
    iota_col = lax.broadcasted_iota(jnp.int32, (rows, 1), 0)
    seg_row, seg_col = jnp.zeros_like(iota_row), jnp.zeros_like(iota_col)
    for i in range(nblk):
        end = jnp.int32(i * block)
        for j in range(nseg):
            end = end + extents[mp * nblk + i, j]
            seg_row = seg_row + (iota_row >= end).astype(jnp.int32)
            seg_col = seg_col + (iota_col >= end).astype(jnp.int32)
    scale = HEAD ** (-0.5)

    @pl.loop(0, nmp)
    def _(i):
        r, slot = 3 - i, lax.rem(i, 2)
        for copy in attn_loads(i):
            copy.wait()

        @pl.when(i + 1 < nmp)
        def _():
            for copy in attn_loads(i + 1):
                copy.start()

        d_mixed = dot(d_attn[...], w_out[slot], 1, 1).astype(BF16)
        for h in range(feat // HEAD):
            lanes = slice(h * HEAD, (h + 1) * HEAD)
            q = qkv[slot, 0, :, lanes] * BF16(scale)
            k = qkv[slot, 1, :, lanes]
            v = qkv[slot, 2, :, lanes]
            d_o = d_mixed[:, lanes]
            scores = jnp.where(seg_col == seg_row, dot(q, k, 1, 1), masked_score)
            expo = jnp.exp(scores - jnp.max(scores, axis=1, keepdims=True))
            probs = expo * (1.0 / jnp.sum(expo, axis=1, keepdims=True))
            d_p = dot(d_o, v, 1, 1)
            d_s = (probs * (d_p - jnp.sum(d_p * probs, axis=1, keepdims=True))).astype(BF16)
            d_proj[:, h * HEAD : (h + 1) * HEAD] = (dot(d_s, k, 1, 0) * scale).astype(BF16)
            d_proj[:, feat + h * HEAD : feat + (h + 1) * HEAD] = dot(d_s, q, 0, 0).astype(BF16)
            d_proj[:, 2 * feat + h * HEAD : 2 * feat + (h + 1) * HEAD] = dot(probs.astype(BF16), d_o, 0, 0).astype(BF16)
        small = parts.shape[3]
        store(2, r, 0, dot(mixed[slot], d_attn[...], 0, 0))
        store(2, r, feat // small, dot(d_proj[...], x[...], 0, 0))
        exchange(2, r)
        vec[r, 6:7, : 3 * feat] = jnp.sum(d_proj[...].astype(F32), axis=0, keepdims=True)
        value = total[...]
        for j in range(3):
            value = value + dot(d_proj[:, j * feat : (j + 1) * feat], w_qkv[slot, j], 1, 0)
        total[...] = value

        @pl.loop(4 + 3 * ((i + 2) // 3) + i // 2 + 2 * (i // 3), 7 + i + i // 2 + i // 3)
        def _(n):
            tick(n)

    for copy in vec_near:
        copy.start()
    low_tok[...] = total[...].astype(BF16)
    tok_near.start()
    tok_own.start()
    for copy in vec_near:
        copy.wait_recv()
    vec_b[...] = vec[2] + vec_a[1]
    vec_far.start()
    vec_s[0] = vec[0] + vec_a[0]
    tok_far.start()

    @pl.loop(12, count + LAGS[6] + extra)
    def _(i):
        @pl.when(i == count)
        def _():
            vec_far.wait()
            vec_s[0] = vec_s[0] + vec_r[0]
            vec_dp[0].start()

        for b in range(bits):
            @pl.when(i == count + 1 + b)
            def _(b=b):
                vec_dp[b].wait()
                value = vec_s[b] + vec_r[1 + b]
                if b + 1 < bits:
                    vec_s[b + 1] = value
                    vec_dp[b + 1].start()
                else:
                    vec_out[...] = value

        tick(i)

    tok_far.wait_recv()
    tok_pass.start()
    for copy in vec_near:
        copy.wait_send()
    for k in range(KINDS):
        for j in range(2):
            near_copy(k, j).wait_send()

    @pl.loop(0, count)
    def _(c):
        for copy in (far_copy, x_copy, p_copy, q_copy, gq_copy, gp_copy, gx_copy):
            copy(c).wait_send()

    tok_near.wait()
    tok_far.wait_send()
    tok_own.wait()
    tok_pass.wait()


def backward(
    d_query, extents, gain1, gain2, upstream, n1, inv1, n2, inv2, h1_low, act, slope, w_up, w_down,
    qkv, mixed, w_out, w_qkv, x, ndp, nmp, block,
):
    rows, wide = x.shape
    feat, hidden = mixed.shape[2], act.shape[2]
    count = KINDS * CHUNKS
    pieces = CHUNKS * PIECES
    small = wide // pieces
    bits = ndp.bit_length() - 1
    extra = max(bits - 3, 1)
    vmem, anywhere = pl.BlockSpec(memory_space=pltpu.VMEM), pl.BlockSpec(memory_space=pl.ANY)
    dma = pltpu.SemaphoreType.DMA
    sds = jax.ShapeDtypeStruct
    vec = (8, wide)
    low, full = (lambda *shape: pltpu.VMEM(shape, BF16)), (lambda *shape: pltpu.VMEM(shape, F32))
    two = lambda a: low(2, *a.shape[1:])
    pair = lambda *shape: [dma(shape), dma(shape)]
    scratch = [full(rows, wide), full(*n1.shape), full(*inv1.shape), full(*n2.shape), full(*inv2.shape)]
    scratch += [low(rows, wide), low(rows, wide), low(*act.shape), two(slope), two(w_up), two(w_down)]
    scratch += [two(qkv), two(mixed), two(w_out), two(w_qkv)]
    scratch += [low(rows, wide), low(rows, wide), low(rows, 3 * feat), low(rows, wide)]
    scratch += [low(KINDS, nmp, pieces, small, wide), full(nmp, *vec), low(KINDS, 2, pieces, small, wide)]
    scratch += [low(count, n, small, wide) for n in (8, 4, 2, 1)] + [low(extra, count, 1, small, wide)]
    scratch += [full(2, *vec), full(*vec), full(bits, *vec), full(bits + 1, *vec)]
    scratch += [dma((8,)), dma((2, 3)), dma((2, 4))]
    scratch += pair(2 * KINDS) + pair(count) * 4 + pair(extra, count) + pair(count) * 3
    scratch += pair(2) + pair(bits + 1) + pair(3) + [dma]
    out = pl.pallas_call(
        functools.partial(backward_kernel, ndp, nmp, block),
        out_shape=(sds((count, 2, 2, 2, small, wide), BF16), sds(vec, F32), sds((nmp, rows, wide), BF16)),
        in_specs=[vmem, pl.BlockSpec(memory_space=pltpu.SMEM), vmem, vmem] + [anywhere] * 15,
        out_specs=(vmem, vmem, anywhere),
        scratch_shapes=scratch,
        compiler_params=pltpu.CompilerParams(
            collective_id=1, has_side_effects=True, vmem_limit_bytes=67043328
        ),
        name="backward",
    )(
        d_query, extents, gain1, gain2, upstream, n1, inv1, n2, inv2, h1_low, act, slope, w_up, w_down,
        qkv, mixed, w_out, w_qkv, x,
    )
    return out[0].reshape(KINDS, wide, wide), out[1], out[2].reshape(-1, wide)


def local(
    encoder_rows,
    piece_extent_sequence,
    triple_projection_matrix,
    asker_content_shifts,
    mixing_result_matrix,
    mixing_result_offset_vector,
    mixing_normalizer_scale,
    mixing_normalizer_shift,
    widen_matrix,
    widen_shift_vector,
    narrow_matrix,
    narrow_shift_vector,
    perceptron_normalizer_scale,
    perceptron_normalizer_shift,
    document_vectors,
    sharpness_factor,
    correct_document_position,
    upstream_sensitivity,
    *,
    width,
    depth,
):
    nblock = piece_extent_sequence.shape[0]
    block = encoder_rows.shape[0] // nblock
    rows = encoder_rows.shape[0] // width
    feat = triple_projection_matrix.shape[2]
    hidden = widen_matrix.shape[1]
    wide = encoder_rows.shape[1]

    w_qkv = triple_projection_matrix.transpose(0, 2, 1)
    small = jnp.concatenate(
        [jnp.pad(asker_content_shifts, ((0, 0), (0, hidden - feat))), widen_shift_vector[None]]
    )
    (
        qkv, mixed, n1, inv1, n2, inv2, h1_low, act, slope, w_qkv, w_out, w_up, w_down, own_out, query, x,
    ) = encode(
        encoder_rows, piece_extent_sequence, w_qkv, mixing_result_matrix, widen_matrix,
        narrow_matrix, small, mixing_result_offset_vector, mixing_normalizer_scale, mixing_normalizer_shift,
        narrow_shift_vector, perceptron_normalizer_scale, perceptron_normalizer_shift, block, width,
    )
    d_query, seg_loss, sharpness_derivative, layer_out = retrieval(
        query, own_out, document_vectors, correct_document_position[None], sharpness_factor, depth, width
    )
    layer_out = layer_out.reshape(-1, wide)
    sums, vectors, grad_tokens = backward(
        d_query, piece_extent_sequence, mixing_normalizer_scale, perceptron_normalizer_scale, upstream_sensitivity, n1, inv1, n2, inv2, h1_low, act, slope,
        w_up, w_down, qkv, mixed, w_out, w_qkv, x, depth, width, block,
    )
    grad_tokens = grad_tokens.astype(F32)
    grad_qkv = sums[2, feat:].astype(F32).reshape(3, feat, wide).transpose(0, 2, 1)
    return (
        layer_out,
        seg_loss[0],
        grad_tokens,
        grad_qkv,
        jnp.stack([vectors[6, :feat], vectors[6, 2 * feat : 3 * feat]]),
        sums[2, :feat].astype(F32),
        vectors[0],
        vectors[1],
        vectors[2],
        sums[1].astype(F32),
        vectors[7, :hidden],
        sums[0].astype(F32),
        vectors[3],
        vectors[4],
        vectors[5],
        sharpness_derivative[0],
    )


def solution(mesh):
    in_specs = (
        P("dp", None),
        P("dp", None),
        P(None, None, "mp"),
        P(None, "mp"),
        P("mp", None),
        P(),
        P(),
        P(),
        P(None, "mp"),
        P("mp"),
        P("mp", None),
        P(),
        P(),
        P(),
        P(("dp", "mp"), None),
        P(),
        P(),
        P("dp", None),
    )
    out_specs = (
        P("dp", None),
        P(),
        P("dp", None),
        P(None, None, "mp"),
        P(None, "mp"),
        P("mp", None),
        P(),
        P(),
        P(),
        P(None, "mp"),
        P("mp"),
        P("mp", None),
        P(),
        P(),
        P(),
        P(),
    )
    width = mesh.shape["mp"]

    def step(*args):
        return local(*args, width=width, depth=mesh.shape["dp"])

    return jax.shard_map(step, mesh=mesh, in_specs=in_specs, out_specs=out_specs, check_vma=False)
```

profile of v0, /device:TPU:0, one launch (start us, length us, event | category | flops | bytes accessed | tf_op | source)
XLA Modules:
  0.0 261.5 jit_solution(8480553951530959149)
XLA Ops:
  1.3 0.7 broadcast_in_dim.6
  2.0 1.3 select_maximum_fusion.refs_6_
  3.3 65.1 %encode.1 = (bf16[4,3,512,192]{3,2,1,0:T(8,128)(2,1)}, bf16[4,512,192]{2,1,0:T(8,128)(2,1)}, f32[512,768]{1,0:T(8,128)}, f32[512,128]{1,0:T(8,128)}, f32[512,768...) custom-call(bf16[2048,768]{1,0:T(8,128)(2,1)} %refs_0_.1, ...), custom_call_target="tpu_custom_call" | custom-call | tf_op jit(solution)/shard_map/encode/pallas_call | solution.py:519
  68.3 43.0 %retrieval.1 = (f32[8,768]{1,0:T(8,128)}, f32[1,256]{1,0:T(1,128)}, f32[1,1]{1,0:T(1,128)}, bf16[4,512,768]{2,1,0:T(8,128)(2,1)}) custom-call(bf16[8,768]{1,0:T(8,128)(2,1)} %get-tuple-element.39.query_ref, bf16[512,768]{1,0:T(8,128)(2,1)} %get-tuple-element.40.own_ref, bf16[4096,768]{1,0:T(8,128)(2,1)} %docs_hbm.1, s32[1,256]{1,0:T(1,128)} %bitcast.45, ...), custom_call_target="tpu_custom_call" | custom-call | tf_op jit(solution)/shard_map/retrieval/pallas_call | solution.py:189
  111.4 132.2 %backward.1 = (bf16[18,2,2,2,16,768]{5,4,3,2,1,0:T(8,128)(2,1)}, f32[8,768]{1,0:T(8,128)}, bf16[4,512,768]{2,1,0:T(8,128)(2,1)}) custom-call(f32[8,768]{1,0:T(8,128)} %get-tuple-element.43.refs_0_, s32[4,8]{1,0:T(4,128)} %refs_1_.3, f32[768]{0:T(1024)} %refs_2_.1, f32[768]{0:T(1024)} %refs_3_.1, f32[2048,768]{1,0:T(8,128)} %refs_4_.1, ...), custom_call_target="tpu_custom_call" | custom-call | tf_op jit(solution)/shard_map/backward/pallas_call | solution.py:944
  243.5 0.0 copy-start
  243.5 0.9 fusion.2
  244.4 0.6 pad_maximum_fusion
  245.0 1.7 slice_reduce_fusion
  246.7 1.8 fusion
  248.5 1.2 slice.54
  249.7 1.4 convert_bitcast_fusion
  251.1 0.0 copy-done
  251.1 0.2 fusion.1
  251.3 0.0 copy-start.2
  251.3 2.7 %bitcast_convert_fusion.1 = (f32[768,768]{1,0:T(8,128)}, f32[768,768]{1,0:T(8,128)}) fusion(bf16[6,2,2,2,16,768]{5,4,3,2,1,0:T(8,128)(2,1)S(1)} %get-tuple-element.69, bf16[6,2,2,2,16,768]{5,4,3,2,1,0:T(8,128)(2,1)S(1)} %get-tuple-element.70), kind=kLoop, calls=%fused_computation.2 | loop fusion | flops 1179648 | bytes 7077888 | tf_op jit(solution)/shard_map/convert_element_type | solution.py:1024
  254.0 0.2 copy-done.2
  254.2 0.0 copy-start.1
  254.2 3.4 %bitcast_convert_fusion = f32[2048,768]{1,0:T(8,128)} fusion(bf16[4,512,768]{2,1,0:T(8,128)(2,1)S(1)} %copy-done.2), kind=kLoop, calls=%fused_computation | loop fusion | flops 1572864 | bytes 9437184 | tf_op jit(solution)/shard_map/convert_element_type | solution.py:1010
  257.6 0.0 copy-done.1
  257.6 0.0 copy-start.3
  257.6 1.7 copy.38
  259.3 0.0 copy-done.3
  259.3 0.6 copy.39
Async XLA Ops:
  243.5 7.5 %copy-start = (bf16[18,2,2,2,16,768]{5,4,3,2,1,0:T(8,128)(2,1)S(1)}, bf16[18,2,2,2,16,768]{5,4,3,2,1,0:T(8,128)(2,1)}, u32[]{:S(2)}) copy-start(bf16[18,2,2,2,16,768]{5,4,3,2,1,0:T(8,128)(2,1)} %get-tuple-element.59) | copy-start | bytes 10616836
  251.3 2.9 %copy-start.2 = (bf16[4,512,768]{2,1,0:T(8,128)(2,1)S(1)}, bf16[4,512,768]{2,1,0:T(8,128)(2,1)}, u32[]{:S(2)}) copy-start(bf16[4,512,768]{2,1,0:T(8,128)(2,1)} %get-tuple-element.58) | copy-start | bytes 9437188
  254.2 3.4 %copy-start.1 = (bf16[4,512,768]{2,1,0:T(8,128)(2,1)S(1)}, bf16[4,512,768]{2,1,0:T(8,128)(2,1)}, u32[]{:S(2)}) copy-start(bf16[4,512,768]{2,1,0:T(8,128)(2,1)} %get-tuple-element.41) | copy-start | bytes 9437188
  257.6 1.7 copy-start.3
where the time goes:
time: 262 us
  Pallas kernels  240 us (92%)
  other arithmetic  11.1 us (4%)
  local copies, waits for them, and re-layouts  7.13 us (3%)
  between operations  3.03 us (1%)
    pallas_call x1, Pallas kernels, backward(): pl.pallas_call(functools.partial(backward_kernel, ndp, nmp, block), out_s...  132 us
    pallas_call x1, Pallas kernels, encode(): pl.pallas_call(functools.partial(encode_kernel, nmp, block), out_shape=tu...  65.1 us
    pallas_call x1, Pallas kernels, retrieval(): pl.pallas_call(functools.partial(retrieval_kernel, ndp, nmp), out_shape=(...  43 us

commit v1 on v0

--- a/solution.py
+++ b/solution.py
@@ -536,7 +536,8 @@
 PIECES = 8
 CHUNKS = 6
 KINDS = 3
-LAGS = (0, 2, 3, 5, 6, 8, 10)
+PACE = 2
+LAGS = (0, 4, 7, 10, 13, 16, 20)
 
 
 def backward_kernel(ndp, nmp, block, *refs):
@@ -668,30 +669,32 @@
 
     def tick(i):
         def at(lag, do):
-            @pl.when((i >= lag) & (i - lag < count))
+            since = i - lag
+
+            @pl.when((since >= 0) & (since < PACE * count) & (lax.rem(since, PACE) == 0))
             def _():
-                do(i - lag)
+                do(since // PACE)
 
         def update(c, first, many, got):
             target = part(c, 0, first, many)
             target[...] = add(target[...], got[c])
 
-        @functools.partial(at, LAGS[6] + extra)
+        @functools.partial(at, LAGS[6] + PACE * extra)
         def _(c):
             gx_copy(c).wait_recv()
 
-        @functools.partial(at, LAGS[5] + extra)
+        @functools.partial(at, LAGS[5] + PACE * extra)
         def _(c):
             gp_copy(c).wait_recv()
             gx_copy(c).start()
 
-        @functools.partial(at, LAGS[4] + extra)
+        @functools.partial(at, LAGS[4] + PACE * extra)
         def _(c):
             gq_copy(c).wait_recv()
             gp_copy(c).start()
 
         for e in reversed(range(extra)):
-            @functools.partial(at, LAGS[3] + 1 + e)
+            @functools.partial(at, LAGS[3] + PACE * (1 + e))
             def _(c, e=e):
                 e_copy(c, e).wait()
                 update(c, ident, 1, got_e.at[e])
@@ -791,7 +794,7 @@
         exchange(1, r)
         total[...] += dot(d_up, w_up[slot], 1, 1)
 
-        @pl.loop(i - (i + 2) // 3, i + i // 3)
+        @pl.loop(PACE * (i - (i + 2) // 3), PACE * (i + i // 3))
         def _(n):
             tick(n)
 
@@ -857,7 +860,7 @@
             value = value + dot(d_proj[:, j * feat : (j + 1) * feat], w_qkv[slot, j], 1, 0)
         total[...] = value
 
-        @pl.loop(4 + 3 * ((i + 2) // 3) + i // 2 + 2 * (i // 3), 7 + i + i // 2 + i // 3)
+        @pl.loop(PACE * (4 + 3 * ((i + 2) // 3) + i // 2 + 2 * (i // 3)), PACE * (7 + i + i // 2 + i // 3))
         def _(n):
             tick(n)
 
@@ -873,16 +876,16 @@
     vec_s[0] = vec[0] + vec_a[0]
     tok_far.start()
 
-    @pl.loop(12, count + LAGS[6] + extra)
+    @pl.loop(PACE * 12, PACE * (count - 1 + extra) + LAGS[6] + 1)
     def _(i):
-        @pl.when(i == count)
+        @pl.when(i == PACE * count)
         def _():
             vec_far.wait()
             vec_s[0] = vec_s[0] + vec_r[0]
             vec_dp[0].start()
 
         for b in range(bits):
-            @pl.when(i == count + 1 + b)
+            @pl.when(i == PACE * (count + 1 + b))
             def _(b=b):
                 vec_dp[b].wait()
                 value = vec_s[b] + vec_r[1 + b]

time: 262 us -> 256 us (0.977)
  Pallas kernels: 240 us -> 234 us
    pallas_call x1, Pallas kernels: 132 us -> 126 us  [backward(): pl.pallas_call(functools.partial(backward_kernel, ndp, nmp, block), out_s...]
where the time goes in v1:
time: 256 us; the launch traced here: 255 us
  Pallas kernels  234 us (91%)
  other arithmetic  11.1 us (4%)
  local copies, waits for them, and re-layouts  7.13 us (3%)
  between operations  3.03 us (1%)
    pallas_call x1, Pallas kernels, backward(): pl.pallas_call(functools.partial(backward_kernel, ndp, nmp, block), out_s...  126 us
    pallas_call x1, Pallas kernels, encode(): pl.pallas_call(functools.partial(encode_kernel, nmp, block), out_shape=tu...  65.1 us
    pallas_call x1, Pallas kernels, retrieval(): pl.pallas_call(functools.partial(retrieval_kernel, ndp, nmp), out_shape=(...  43 us

profile of v1, /device:TPU:0, one launch (start us, length us, event | category | flops | bytes accessed | tf_op | source)
XLA Modules:
  0.0 255.2 jit_solution(9913489302474831524)
XLA Ops:
  1.3 0.7 broadcast_in_dim.6
  2.0 1.3 select_maximum_fusion.refs_6_
  3.3 65.1 %encode.1 = (bf16[4,3,512,192]{3,2,1,0:T(8,128)(2,1)}, bf16[4,512,192]{2,1,0:T(8,128)(2,1)}, f32[512,768]{1,0:T(8,128)}, f32[512,128]{1,0:T(8,128)}, f32[512,768...) custom-call(bf16[2048,768]{1,0:T(8,128)(2,1)} %refs_0_.1, ...), custom_call_target="tpu_custom_call" | custom-call | tf_op jit(solution)/shard_map/encode/pallas_call | solution.py:519
  68.3 43.0 %retrieval.1 = (f32[8,768]{1,0:T(8,128)}, f32[1,256]{1,0:T(1,128)}, f32[1,1]{1,0:T(1,128)}, bf16[4,512,768]{2,1,0:T(8,128)(2,1)}) custom-call(bf16[8,768]{1,0:T(8,128)(2,1)} %get-tuple-element.39.query_ref, bf16[512,768]{1,0:T(8,128)(2,1)} %get-tuple-element.40.own_ref, bf16[4096,768]{1,0:T(8,128)(2,1)} %docs_hbm.1, s32[1,256]{1,0:T(1,128)} %bitcast.45, ...), custom_call_target="tpu_custom_call" | custom-call | tf_op jit(solution)/shard_map/retrieval/pallas_call | solution.py:189
  111.4 125.9 %backward.1 = (bf16[18,2,2,2,16,768]{5,4,3,2,1,0:T(8,128)(2,1)}, f32[8,768]{1,0:T(8,128)}, bf16[4,512,768]{2,1,0:T(8,128)(2,1)}) custom-call(f32[8,768]{1,0:T(8,128)} %get-tuple-element.43.refs_0_, s32[4,8]{1,0:T(4,128)} %refs_1_.3, f32[768]{0:T(1024)} %refs_2_.1, f32[768]{0:T(1024)} %refs_3_.1, f32[2048,768]{1,0:T(8,128)} %refs_4_.1, ...), custom_call_target="tpu_custom_call" | custom-call | tf_op jit(solution)/shard_map/backward/pallas_call | solution.py:947
  237.2 0.0 copy-start
  237.3 0.9 fusion.2
  238.1 0.6 pad_maximum_fusion
  238.7 1.7 slice_reduce_fusion
  240.4 1.8 fusion
  242.2 1.2 slice.54
  243.4 1.4 convert_bitcast_fusion
  244.8 0.0 copy-done
  244.8 0.2 fusion.1
  245.0 0.0 copy-start.2
  245.0 2.7 %bitcast_convert_fusion.1 = (f32[768,768]{1,0:T(8,128)}, f32[768,768]{1,0:T(8,128)}) fusion(bf16[6,2,2,2,16,768]{5,4,3,2,1,0:T(8,128)(2,1)S(1)} %get-tuple-element.69, bf16[6,2,2,2,16,768]{5,4,3,2,1,0:T(8,128)(2,1)S(1)} %get-tuple-element.70), kind=kLoop, calls=%fused_computation.2 | loop fusion | flops 1179648 | bytes 7077888 | tf_op jit(solution)/shard_map/convert_element_type | solution.py:1027
  247.7 0.2 copy-done.2
  247.9 0.0 copy-start.1
  247.9 3.4 %bitcast_convert_fusion = f32[2048,768]{1,0:T(8,128)} fusion(bf16[4,512,768]{2,1,0:T(8,128)(2,1)S(1)} %copy-done.2), kind=kLoop, calls=%fused_computation | loop fusion | flops 1572864 | bytes 9437184 | tf_op jit(solution)/shard_map/convert_element_type | solution.py:1013
  251.3 0.0 copy-done.1
  251.3 0.0 copy-start.3
  251.3 1.7 copy.38
  253.0 0.0 copy-done.3
  253.0 0.6 copy.39
Async XLA Ops:
  237.2 7.5 %copy-start = (bf16[18,2,2,2,16,768]{5,4,3,2,1,0:T(8,128)(2,1)S(1)}, bf16[18,2,2,2,16,768]{5,4,3,2,1,0:T(8,128)(2,1)}, u32[]{:S(2)}) copy-start(bf16[18,2,2,2,16,768]{5,4,3,2,1,0:T(8,128)(2,1)} %get-tuple-element.59) | copy-start | bytes 10616836
  245.0 2.9 %copy-start.2 = (bf16[4,512,768]{2,1,0:T(8,128)(2,1)S(1)}, bf16[4,512,768]{2,1,0:T(8,128)(2,1)}, u32[]{:S(2)}) copy-start(bf16[4,512,768]{2,1,0:T(8,128)(2,1)} %get-tuple-element.58) | copy-start | bytes 9437188
  247.9 3.4 %copy-start.1 = (bf16[4,512,768]{2,1,0:T(8,128)(2,1)S(1)}, bf16[4,512,768]{2,1,0:T(8,128)(2,1)}, u32[]{:S(2)}) copy-start(bf16[4,512,768]{2,1,0:T(8,128)(2,1)} %get-tuple-element.41) | copy-start | bytes 9437188
  251.3 1.7 copy-start.3

commit v2 on v1

--- a/solution.py
+++ b/solution.py
@@ -536,8 +536,8 @@
 PIECES = 8
 CHUNKS = 6
 KINDS = 3
-PACE = 2
-LAGS = (0, 4, 7, 10, 13, 16, 20)
+PACE = 4
+LAGS = (0, 7, 12, 18, 24, 29, 36)
 
 
 def backward_kernel(ndp, nmp, block, *refs):

time: 256 us -> 257 us (level)
  no operation moved by 1% of the time
where the time goes in v2:
time: 257 us
  Pallas kernels  236 us (92%)
  other arithmetic  11.1 us (4%)
  local copies, waits for them, and re-layouts  7.13 us (3%)
  between operations  3.03 us (1%)
    pallas_call x1, Pallas kernels, backward(): pl.pallas_call(functools.partial(backward_kernel, ndp, nmp, block), out_s...  128 us
    pallas_call x1, Pallas kernels, encode(): pl.pallas_call(functools.partial(encode_kernel, nmp, block), out_shape=tu...  65.1 us
    pallas_call x1, Pallas kernels, retrieval(): pl.pallas_call(functools.partial(retrieval_kernel, ndp, nmp), out_shape=(...  43 us

profile of v2, /device:TPU:0, one launch (start us, length us, event | category | flops | bytes accessed | tf_op | source)
XLA Modules:
  0.0 257.0 jit_solution(5901086960031822294)
XLA Ops:
  1.3 0.7 broadcast_in_dim.6
  2.0 1.3 select_maximum_fusion.refs_6_
  3.3 65.1 %encode.1 = (bf16[4,3,512,192]{3,2,1,0:T(8,128)(2,1)}, bf16[4,512,192]{2,1,0:T(8,128)(2,1)}, f32[512,768]{1,0:T(8,128)}, f32[512,128]{1,0:T(8,128)}, f32[512,768...) custom-call(bf16[2048,768]{1,0:T(8,128)(2,1)} %refs_0_.1, ...), custom_call_target="tpu_custom_call" | custom-call | tf_op jit(solution)/shard_map/encode/pallas_call | solution.py:519
  68.3 43.0 %retrieval.1 = (f32[8,768]{1,0:T(8,128)}, f32[1,256]{1,0:T(1,128)}, f32[1,1]{1,0:T(1,128)}, bf16[4,512,768]{2,1,0:T(8,128)(2,1)}) custom-call(bf16[8,768]{1,0:T(8,128)(2,1)} %get-tuple-element.39.query_ref, bf16[512,768]{1,0:T(8,128)(2,1)} %get-tuple-element.40.own_ref, bf16[4096,768]{1,0:T(8,128)(2,1)} %docs_hbm.1, s32[1,256]{1,0:T(1,128)} %bitcast.45, ...), custom_call_target="tpu_custom_call" | custom-call | tf_op jit(solution)/shard_map/retrieval/pallas_call | solution.py:189
  111.4 127.6 %backward.1 = (bf16[18,2,2,2,16,768]{5,4,3,2,1,0:T(8,128)(2,1)}, f32[8,768]{1,0:T(8,128)}, bf16[4,512,768]{2,1,0:T(8,128)(2,1)}) custom-call(f32[8,768]{1,0:T(8,128)} %get-tuple-element.43.refs_0_, s32[4,8]{1,0:T(4,128)} %refs_1_.3, f32[768]{0:T(1024)} %refs_2_.1, f32[768]{0:T(1024)} %refs_3_.1, f32[2048,768]{1,0:T(8,128)} %refs_4_.1, ...), custom_call_target="tpu_custom_call" | custom-call | tf_op jit(solution)/shard_map/backward/pallas_call | solution.py:947
  239.0 0.0 copy-start
  239.0 0.9 fusion.2
  239.8 0.6 pad_maximum_fusion
  240.4 1.7 slice_reduce_fusion
  242.1 1.8 fusion
  243.9 1.2 slice.54
  245.1 1.4 convert_bitcast_fusion
  246.5 0.0 copy-done
  246.5 0.2 fusion.1
  246.7 0.0 copy-start.2
  246.7 2.7 %bitcast_convert_fusion.1 = (f32[768,768]{1,0:T(8,128)}, f32[768,768]{1,0:T(8,128)}) fusion(bf16[6,2,2,2,16,768]{5,4,3,2,1,0:T(8,128)(2,1)S(1)} %get-tuple-element.69, bf16[6,2,2,2,16,768]{5,4,3,2,1,0:T(8,128)(2,1)S(1)} %get-tuple-element.70), kind=kLoop, calls=%fused_computation.2 | loop fusion | flops 1179648 | bytes 7077888 | tf_op jit(solution)/shard_map/convert_element_type | solution.py:1027
  249.4 0.2 copy-done.2
  249.6 0.0 copy-start.1
  249.7 3.4 %bitcast_convert_fusion = f32[2048,768]{1,0:T(8,128)} fusion(bf16[4,512,768]{2,1,0:T(8,128)(2,1)S(1)} %copy-done.2), kind=kLoop, calls=%fused_computation | loop fusion | flops 1572864 | bytes 9437184 | tf_op jit(solution)/shard_map/convert_element_type | solution.py:1013
  253.0 0.0 copy-done.1
  253.0 0.0 copy-start.3
  253.0 1.7 copy.38
  254.7 0.0 copy-done.3
  254.7 0.6 copy.39
Async XLA Ops:
  239.0 7.5 %copy-start = (bf16[18,2,2,2,16,768]{5,4,3,2,1,0:T(8,128)(2,1)S(1)}, bf16[18,2,2,2,16,768]{5,4,3,2,1,0:T(8,128)(2,1)}, u32[]{:S(2)}) copy-start(bf16[18,2,2,2,16,768]{5,4,3,2,1,0:T(8,128)(2,1)} %get-tuple-element.59) | copy-start | bytes 10616836
  246.7 2.9 %copy-start.2 = (bf16[4,512,768]{2,1,0:T(8,128)(2,1)S(1)}, bf16[4,512,768]{2,1,0:T(8,128)(2,1)}, u32[]{:S(2)}) copy-start(bf16[4,512,768]{2,1,0:T(8,128)(2,1)} %get-tuple-element.58) | copy-start | bytes 9437188
  249.6 3.4 %copy-start.1 = (bf16[4,512,768]{2,1,0:T(8,128)(2,1)S(1)}, bf16[4,512,768]{2,1,0:T(8,128)(2,1)}, u32[]{:S(2)}) copy-start(bf16[4,512,768]{2,1,0:T(8,128)(2,1)} %get-tuple-element.41) | copy-start | bytes 9437188
  253.0 1.7 copy-start.3
